TPU v7x, 32 devices: a whole 2x2x4 slice. The times are simulated.
32 devices in a mesh: group: 2 (over y), ep: 4 (over x, core), tp: 4 (over z).
Axes of the slice: x: 2, y: 2, z: 4, core: 2. Of those that a mesh axis runs over, the one named last changes fastest.
Arguments:
- tokens: bfloat16 [192, 3072], P(('group', 'ep', 'tp')), parts along dimension 0, may hold values from -6 to 6
- experts: int32 [192, 2], P(('group', 'ep', 'tp')), parts along dimension 0, may hold values from 0 to 3, as said below
- replicas: int32 [192, 2], P(('group', 'ep', 'tp')), parts along dimension 0, may hold values from 0 to 2, as said below
- gates: float32 [192, 2], P(('group', 'ep', 'tp')), parts along dimension 0, may hold values from 0.1 to 1
- w_gate: bfloat16 [16, 3072, 4096], P('ep', None, 'tp'), may hold values from -0.109375 to 0.109375
- w_up: bfloat16 [16, 3072, 4096], P('ep', None, 'tp'), may hold values from -0.109375 to 0.109375
- w_down: bfloat16 [16, 4096, 3072], P('ep', 'tp'), may hold values from -0.0625 to 0.0625
Outputs:
- moe_output: bfloat16 [192, 3072], P(('group', 'ep', 'tp')), parts along dimension 0
There are 2 independent parts, one for each index of `group`. A program takes and returns all parts, laid end to end along the dimension named above; an argument that names none is the same for every part. Nothing has to cross between parts.
Inputs may be any that keep to these rules, and one draw needn't show every extreme that they name: The two experts of a row differ. `replicas`: a replica above 0 stands only beside an expert below 2; the picks of the rows of one device name one instance at most 2 times, exactly 2 times for some instance on every device; the picks of the rows of all devices with one index of tp name one instance at most 8 times, exactly 8 times for some instance.
All inputs are finite; a program needn't handle non-finite values.
Results may differ from a plain program's by a relative error of at most 0.018.
Values may be sent and summed in bfloat16 or wider, within the bound.
No kernel may reach another device: no remote copies, remote signals or barrier semaphores. Data moves between devices by JAX's collectives and lax.ppermute only.
A program may use at most 128 MiB of HBM per device.

v0:
```python
import jax
import jax.numpy as jnp
from jax import lax
from jax.sharding import PartitionSpec as P

SPLIT = 2
CAP = 2


def pack_rows(arrived, arrived_flags, recv_most):
    src_count, local_piece, col_count, depth = arrived_flags.shape
    marked = jnp.transpose(arrived_flags.astype(jnp.float32), (2, 1, 0, 3)).reshape(
        col_count, local_piece, src_count * depth
    )
    before = jnp.cumsum(marked, axis=2) - marked
    places = jnp.arange(recv_most, dtype=jnp.float32)
    select = (before[:, :, None, :] == places[None, None, :, None]) & (marked[:, :, None, :] > 0.5)
    select = select.astype(jnp.bfloat16).reshape(
        col_count, local_piece, recv_most, src_count, depth
    )
    packed = jnp.einsum(
        "tqrec,eqtcd->trqd", select, arrived, preferred_element_type=jnp.float32
    ).astype(jnp.bfloat16)
    return (packed.reshape(col_count * recv_most, local_piece, arrived.shape[-1]), select)


def on_device(tokens, experts, replicas, gates, w_gate, w_up, w_down):
    ep_count = lax.axis_size("ep")
    local_piece = w_gate.shape[0]
    piece_count = local_piece * ep_count
    inst_count = piece_count // SPLIT
    expert_count = inst_count // 2
    hot_count = expert_count // 2
    recv_most = CAP * ep_count
    rows_dev, features = tokens.shape
    slot_total = inst_count * CAP
    instance = jnp.where(
        replicas == 0,
        experts,
        expert_count + (replicas - 1) * hot_count + (experts - 1) % hot_count,
    )
    pick_ids = instance.reshape(-1)
    matching = pick_ids[:, None] == pick_ids[None, :]
    positions = jnp.arange(pick_ids.shape[0])
    earlier = positions[:, None] > positions[None, :]
    slot_idx = jnp.sum((matching & earlier).astype(jnp.int32), axis=1)
    target = pick_ids * CAP + slot_idx
    onehot = (jnp.arange(slot_total)[:, None] == target[None, :]).astype(jnp.float32)
    slot_rows = onehot.reshape(slot_total, rows_dev, 2).sum(axis=2)
    inst_rows = jnp.dot(
        slot_rows.astype(jnp.bfloat16), tokens, preferred_element_type=jnp.float32
    ).astype(jnp.bfloat16)
    send_rows = jnp.repeat(inst_rows.reshape(inst_count, CAP, features), SPLIT, axis=0).reshape(
        ep_count, local_piece, CAP, features
    )
    inst_flags = jnp.sum(slot_rows, axis=1).astype(jnp.bfloat16).reshape(inst_count, CAP)
    send_flags = jnp.repeat(inst_flags, SPLIT, axis=0).reshape(ep_count, local_piece, CAP)
    arrived, arrived_flags = (
        lax.all_to_all(send_rows, "ep", split_axis=0, concat_axis=0, tiled=True),
        lax.all_to_all(send_flags, "ep", split_axis=0, concat_axis=0, tiled=True),
    )
    packed, select = pack_rows(arrived[:, :, None], arrived_flags[:, :, None], recv_most)
    own_select = select[0]
    piece = lax.all_gather(packed, "tp", axis=0, tiled=True)
    gate_act = jnp.einsum("rqd,qdf->rqf", piece, w_gate, preferred_element_type=jnp.float32)
    up_act = jnp.einsum("rqd,qdf->rqf", piece, w_up, preferred_element_type=jnp.float32)
    hidden = (jax.nn.silu(gate_act) * up_act).astype(jnp.bfloat16)
    piece = hidden
    summed = lax.psum_scatter(
        jnp.einsum("rqf,qfd->rqd", piece, w_down, preferred_element_type=jnp.float32).astype(
            jnp.bfloat16
        ),
        "tp",
        scatter_dimension=0,
        tiled=True,
    )
    returning = jnp.einsum(
        "qrec,rqd->eqcd", own_select, summed, preferred_element_type=jnp.float32
    ).astype(jnp.bfloat16)
    returned = lax.all_to_all(returning, "ep", split_axis=0, concat_axis=0, tiled=True)
    halves = returned.reshape(inst_count, SPLIT, CAP, features).astype(jnp.float32)
    returned_rows = jnp.sum(halves, axis=1).reshape(slot_total, features)
    weighted = (onehot * gates.reshape(-1)[None, :]).reshape(slot_total, rows_dev, 2).sum(axis=2)
    mixed = jnp.dot(weighted.T, returned_rows, precision=lax.Precision.HIGHEST)
    return mixed.astype(jnp.bfloat16)


def solution(mesh):
    return jax.shard_map(
        on_device,
        mesh=mesh,
        in_specs=(
            P(("group", "ep", "tp"), None),
            P(("group", "ep", "tp"), None),
            P(("group", "ep", "tp"), None),
            P(("group", "ep", "tp"), None),
            P("ep", None, "tp"),
            P("ep", None, "tp"),
            P("ep", "tp", None),
        ),
        out_specs=P(("group", "ep", "tp"), None),
        check_vma=False,
    )
```

profile of v0, /device:TPU:0, one launch (start us, length us, event | category | flops | bytes accessed | tf_op | source)
XLA Modules:
  0.0 119.7 jit_solution(8980640386766301691)
XLA Ops:
  6.5 0.0 copy-start
  6.5 0.8 copy.65
  7.3 0.8 copy.62
  8.1 0.1 eq.55
  8.2 0.2 convert_reduce_fusion.1
  8.4 0.1 reduce_sum.48
  8.4 0.8 copy.66
  9.2 0.1 convert_reduce_fusion.2
  9.3 0.1 convert_element_type.63
  9.4 0.1 copy.67
  9.5 0.1 broadcast_in_dim.5
  9.6 0.1 reshape_reshape.7
  9.7 0.6 copy.68
  10.3 4.2 %all-to-all-start.1 = ((bf16[4,4,2]{1,2,0:T(2,128)(2,1)}), bf16[4,4,2]{1,2,0:T(2,128)(2,1)S(1)}, u32[]{:S(2)}, u32[]{:S(2)}) async-start(bf16[4,4,2]{1,2,0:T(2,128)(2,1)} %copy.68), calls=%async_computation.1 | async-start | bytes 4096 | tf_op jit(solution)/shard_map/all_to_all | solution.py:60
  14.5 0.0 copy-done
  14.5 0.2 convolution_convert_fusion.2
  14.8 3.4 %all-to-all-done.1 = bf16[4,4,2]{1,2,0:T(2,128)(2,1)S(1)} async-done(((bf16[4,4,2]{1,2,0:T(2,128)(2,1)}), bf16[4,4,2]{1,2,0:T(2,128)(2,1)S(1)}, u32[]{:S(2)}, u32[]{:S(2)}) %all-to-all-start.1) | async-done | bytes 96 | tf_op jit(solution)/shard_map/all_to_all | solution.py:60
  18.2 0.8 broadcast_in_dim.4
  19.0 3.4 %all-to-all-start = ((bf16[4,4,2,3072]{3,2,1,0:T(2,128)(2,1)}), bf16[4,4,2,3072]{3,2,1,0:T(2,128)(2,1)S(1)}, u32[]{:S(2)}, u32[]{:S(2)}) async-start(bf16[4,4,2,3072]{3,2,1,0:T(2,128)(2,1)} %bitcast), calls=%async_computation | async-start | bytes 393216 | tf_op jit(solution)/shard_map/all_to_all | solution.py:59
  22.3 0.0 reduce-scatter.4.cloned.1.call-start
  22.4 0.1 copy.71
  22.5 0.1 copy.72
  22.7 0.1 fusion.9
  22.8 4.9 %all-to-all-done = bf16[4,4,2,3072]{3,2,1,0:T(2,128)(2,1)S(1)} async-done(((bf16[4,4,2,3072]{3,2,1,0:T(2,128)(2,1)}), bf16[4,4,2,3072]{3,2,1,0:T(2,128)(2,1)S(1)}, u32[]{:S(2)}, u32[]{:S(2)}) %all-to-all-start) | async-done | bytes 196640 | tf_op jit(solution)/shard_map/all_to_all | solution.py:59
  27.6 0.3 fusion.2
  27.9 20.3 %all-gather = bf16[1,32,4,3072]{3,1,2,0:T(8,128)(2,1)S(1)} all-gather(bf16[1,8,4,3072]{3,1,2,0:T(8,128)(2,1)S(1)} %fusion.2), channel_id=2, replica_groups=mesh['group'=2,'ep'=4,'tp'=4] {'tp'}, dimensions={1}, use_global_device_ids=true | all-gather | bytes 983040 | tf_op jit(solution)/shard_map/all_gather | solution.py:64
  48.2 10.4 %convolution_bitcast_fusion.2 = f32[32,4,1024]{2,0,1:T(8,128)S(1)} fusion(bf16[4,3072,1024]{2,1,0:T(8,128)(2,1)} %param.11, bf16[1,32,4,3072]{3,1,2,0:T(8,128)(2,1)S(1)} %all-gather), kind=kOutput, calls=%fused_computation.10 | convolution fusion | flops 805306368 | bytes 26476544 | tf_op jit(solution)/shard_map/rqd,qdf->rqf/dot_general | solution.py:65
  58.6 10.6 %fusion.5 = bf16[32,4,1024]{2,0,1:T(8,128)(2,1)S(1)} fusion(bf16[4,3072,1024]{2,1,0:T(8,128)(2,1)} %param.12, bf16[1,32,4,3072]{3,1,2,0:T(8,128)(2,1)S(1)} %all-gather, f32[32,4,1024]{2,0,1:T(8,128)S(1)} %convolution_bitcast_fusion.2), kind=kOutput, calls=%fused_computation.12 | convolution fusion | flops 806092800 | bytes 26738688 | tf_op jit(solution)/shard_map/rqd,qdf->rqf/dot_general | solution.py:66
  69.2 10.5 %fusion = bf16[4,4,8,3072]{3,2,1,0:T(8,128)(2,1)S(1)} fusion(bf16[32,4,1024]{2,0,1:T(8,128)(2,1)S(1)} %fusion.5, bf16[4,1024,3072]{2,1,0:T(8,128)(2,1)} %param.13), kind=kOutput, calls=%fused_computation.1 | convolution fusion | flops 805699584 | bytes 26214400 | tf_op jit(solution)/shard_map/rqf,qfd->rqd/dot_general | solution.py:70
  79.8 0.9 copy.80
  80.7 0.0 reduce-scatter.4.cloned.1.call-update
  80.7 21.7 %reduce-scatter.4.cloned.1.call-done = bf16[8,12288]{1,0:T(8,128)(2,1)} async-done(((bf16[32,12288]{1,0:T(8,128)(2,1)}), bf16[8,12288]{1,0:T(8,128)(2,1)}) %reduce-scatter.4.cloned.1.call-update) | async-done | bytes 196624
  102.5 1.2 fusion.3
  103.7 0.2 copy.76
  103.8 7.8 %all_to_all.15 = bf16[4,4,2,3072]{3,2,1,0:T(2,128)(2,1)S(1)} all-to-all(bf16[4,4,2,3072]{3,2,1,0:T(2,128)(2,1)S(1)} %copy.76), channel_id=1, replica_groups=mesh['group'=2,'ep'=4,'tp'=4] {'ep'}, dimensions={0} | all-to-all | bytes 393216 | tf_op jit(solution)/shard_map/all_to_all | solution.py:80
  111.6 0.2 convert_reduce_fusion
  111.8 0.1 reshape.97
  112.0 0.8 convolution_convert_fusion.3
  (10 shorter events, 0.1 us)
Async XLA Ops:
  6.5 8.0 %copy-start = (bf16[6,3072]{1,0:T(8,128)(2,1)S(1)}, bf16[6,3072]{1,0:T(8,128)(2,1)}, u32[]{:S(2)}) copy-start(bf16[6,3072]{1,0:T(8,128)(2,1)} %param.7) | copy-start | bytes 110596
  10.3 7.9 %all-to-all-start.1 = ((bf16[4,4,2]{1,2,0:T(2,128)(2,1)}), bf16[4,4,2]{1,2,0:T(2,128)(2,1)S(1)}, u32[]{:S(2)}, u32[]{:S(2)}) async-start(bf16[4,4,2]{1,2,0:T(2,128)(2,1)} %copy.68), calls=%async_computation.1 | async-start | bytes 4096 | tf_op jit(solution)/shard_map/all_to_all | solution.py:60
  19.0 8.6 %all-to-all-start = ((bf16[4,4,2,3072]{3,2,1,0:T(2,128)(2,1)}), bf16[4,4,2,3072]{3,2,1,0:T(2,128)(2,1)S(1)}, u32[]{:S(2)}, u32[]{:S(2)}) async-start(bf16[4,4,2,3072]{3,2,1,0:T(2,128)(2,1)} %bitcast), calls=%async_computation | async-start | bytes 393216 | tf_op jit(solution)/shard_map/all_to_all | solution.py:59
  22.3 80.1 %reduce-scatter.4.cloned.1.call-start = ((), (), s32[]{:S(2)}) async-start(), calls=%async_computation.4 | async-start | bytes 983040
Sparse Core Ops, SparseCore 0:
  80.9 21.5 reduce-scatter.3
where the time goes:
time: 120 us
  matrix products  34.1 us (28%)
  waiting for transfers between devices  30.1 us (25%)
  blocking collectives  28.1 us (23%)
  between operations  13.5 us (11%)
  starting transfers between devices  7.64 us (6%)
  local copies, waits for them, and re-layouts  5.67 us (5%)
    unnamed x2, waiting for transfers between devices  21.8 us
    all_gather x1, blocking collectives, on_device(): piece = lax.all_gather(packed, 'tp', axis=0, tiled=True)  20.3 us
    dot_general x1, matrix products, on_device(): jnp.einsum('rqd,qdf->rqf', piece, w_up, preferred_element_type=jnp.float32)  10.6 us
    dot_general x1, matrix products, on_device(): jnp.einsum('rqf,qfd->rqd', piece, w_down, preferred_element_type=jnp.floa...  10.5 us
    dot_general x1, matrix products, on_device(): jnp.einsum('rqd,qdf->rqf', piece, w_gate, preferred_element_type=jnp.floa...  10.4 us
    all_to_all x1, blocking collectives, on_device(): lax.all_to_all(returning, 'ep', split_axis=0, concat_axis=0, tiled=True)  7.79 us
    all_to_all x1, waiting for transfers between devices, on_device(): lax.all_to_all(send_rows, 'ep', split_axis=0, concat_axis=0, tiled=True)  4.86 us
    all_to_all x1, starting transfers between devices, on_device(): lax.all_to_all(send_flags, 'ep', split_axis=0, concat_axis=0, tiled=True)  4.24 us
  transfers between devices with their start and end apart: 3, of which 3 were waited for; matrix products, arithmetic and copies ran while one was open for 1% of the time, Pallas kernels for 0%

commit v1 on v0

v1 whole, which is shorter than its diff:
```python
import functools

import jax
import jax.numpy as jnp
from jax import lax
from jax.experimental import pallas as pl
from jax.experimental.pallas import tpu as pltpu
from jax.sharding import PartitionSpec as P

SPLIT = 2
LANES = 128
META = 2


def partner(count, step):
    if count & (count - 1) == 0:
        return [(i, i ^ step) for i in range(count)]
    return [(i, (i + step) % count) for i in range(count)]


def back(count, step):
    return [(dst, src) for src, dst in partner(count, step)]


def stages(count, direct):
    if direct or count & (count - 1) != 0:
        return [list(range(1, count))]
    found, bit = [], count // 2
    while bit >= 1:
        found.append([bit])
        bit //= 2
    return found


def gather(rows, axis, direct):
    count = lax.axis_size(axis)
    for steps in stages(count, direct):
        arrived = [lax.ppermute(rows, axis, partner(count, step)) for step in steps]
        rows = jnp.concatenate([rows] + arrived, axis=0)
    return rows


def scatter_sum(rows, axis, direct):
    count = lax.axis_size(axis)
    for steps in reversed(stages(count, direct)):
        parts = jnp.split(rows, len(steps) + 1, axis=0)
        arrived = [
            lax.ppermute(part, axis, back(count, step)) for part, step in zip(parts[1:], steps)
        ]
        total = parts[0].astype(jnp.float32)
        for part in arrived:
            total = total + part.astype(jnp.float32)
        rows = total.astype(jnp.bfloat16)
    return rows


def pack_kernel(inst_count, tokens, experts, replicas, gates, out, wide):
    rows_dev, features = tokens.shape
    expert_count = inst_count // 2
    hot_count = expert_count // 2
    wide[...] = jnp.zeros_like(wide)
    wide[:rows_dev, :] = tokens[...].astype(jnp.float32)
    picked, copy = experts[...], replicas[...]
    turn = jnp.zeros_like(picked)
    for e in range(expert_count):
        turn = jnp.where(picked == e, (e - 1) % hot_count, turn)
    instance = jnp.where(copy == 0, picked, expert_count + (copy - 1) * hot_count + turn)
    for i in range(inst_count):
        weight = jnp.sum(jnp.where(instance == i, gates[...], 0.0), axis=0, keepdims=True)
        high = weight.astype(jnp.bfloat16).astype(jnp.float32)
        low = (weight - high).astype(jnp.bfloat16).astype(jnp.float32)
        lanes = slice(i * LANES, i * LANES + rows_dev)
        wide[rows_dev : rows_dev + 1, lanes] = high
        wide[rows_dev + 1 : rows_dev + 2, lanes] = low
    out[...] = wide[...].astype(jnp.bfloat16)


def pack(tokens, experts, replicas, gates, inst_count):
    rows_dev, features = tokens.shape
    block = -(-(rows_dev + META) // 8) * 8
    return pl.pallas_call(
        functools.partial(pack_kernel, inst_count),
        out_shape=jax.ShapeDtypeStruct((block, features), jnp.bfloat16),
        scratch_shapes=[pltpu.VMEM((block, features), jnp.float32)],
    )(tokens, experts.T, replicas.T, gates.T)


def expert_kernel(block, rows_dev, first_ref, x, w_gate, w_up, w_down, out, total):
    piece, part = pl.program_id(1), pl.program_id(2)
    tile = x.shape[0]
    begin = (piece == 0) & (part == 0)
    instance = (first_ref[0] + piece) // SPLIT
    lanes = pl.ds(pl.multiple_of(instance * LANES, LANES), LANES)
    slab = x[:, lanes].astype(jnp.float32).reshape(tile // block, block, LANES)
    weight = slab[:, rows_dev : rows_dev + 1, :] + slab[:, rows_dev + 1 : rows_dev + 2, :]
    shape = (tile // block, block, LANES)
    row = lax.broadcasted_iota(jnp.int32, shape, 1)
    lane = lax.broadcasted_iota(jnp.int32, shape, 2)
    own = jnp.where((row == lane) & (row < rows_dev), jnp.broadcast_to(weight, shape), 0.0)
    coef = jnp.sum(own, axis=2, keepdims=True).reshape(tile, 1)
    gate_act = jnp.dot(x[...], w_gate[0], preferred_element_type=jnp.float32)
    up_act = jnp.dot(x[...], w_up[0], preferred_element_type=jnp.float32)
    hidden = (gate_act / (1.0 + jnp.exp(-gate_act)) * up_act * coef).astype(jnp.bfloat16)
    share = jnp.dot(hidden, w_down[0], preferred_element_type=jnp.float32)

    @pl.when(begin)
    def _():
        total[...] = share

    @pl.when(jnp.logical_not(begin))
    def _():
        total[...] += share

    @pl.when((piece == pl.num_programs(1) - 1) & (part == pl.num_programs(2) - 1))
    def _():
        out[...] = total[...].astype(jnp.bfloat16)


def experts_of(x, first, w_gate, w_up, w_down, block, rows_dev):
    rows, features = x.shape
    pieces, _, hidden_dev = w_gate.shape
    width = min(512, hidden_dev)
    tile = min(rows, 128)
    return pl.pallas_call(
        functools.partial(expert_kernel, block, rows_dev),
        out_shape=jax.ShapeDtypeStruct((rows, features), jnp.bfloat16),
        grid_spec=pltpu.PrefetchScalarGridSpec(
            num_scalar_prefetch=1,
            grid=(rows // tile, pieces, hidden_dev // width),
            in_specs=[
                pl.BlockSpec((tile, features), lambda r, q, f, s: (r, 0)),
                pl.BlockSpec((1, features, width), lambda r, q, f, s: (q, 0, f)),
                pl.BlockSpec((1, features, width), lambda r, q, f, s: (q, 0, f)),
                pl.BlockSpec((1, width, features), lambda r, q, f, s: (q, f, 0)),
            ],
            out_specs=pl.BlockSpec((tile, features), lambda r, q, f, s: (r, 0)),
            scratch_shapes=[pltpu.VMEM((tile, features), jnp.float32)],
        ),
        compiler_params=pltpu.CompilerParams(vmem_limit_bytes=40 << 20),
    )(first, x, w_gate, w_up, w_down)


def on_device(tokens, experts, replicas, gates, w_gate, w_up, w_down):
    local_piece = w_gate.shape[0]
    inst_count = local_piece * lax.axis_size("ep") // SPLIT
    rows_dev = tokens.shape[0]
    direct = lax.axis_size("tp") <= 4
    block_rows = pack(tokens, experts, replicas, gates, inst_count)
    block = block_rows.shape[0]
    rows = gather(block_rows, "tp", direct)
    rows = gather(rows, "ep", False)
    first = (lax.axis_index("ep") * local_piece).astype(jnp.int32).reshape(1)
    share = experts_of(rows, first, w_gate, w_up, w_down, block, rows_dev)
    share = scatter_sum(share, "ep", False)
    share = scatter_sum(share, "tp", direct)
    return share[:rows_dev]


def solution(mesh):
    return jax.shard_map(
        on_device,
        mesh=mesh,
        in_specs=(
            P(("group", "ep", "tp"), None),
            P(("group", "ep", "tp"), None),
            P(("group", "ep", "tp"), None),
            P(("group", "ep", "tp"), None),
            P("ep", None, "tp"),
            P("ep", None, "tp"),
            P("ep", "tp", None),
        ),
        out_specs=P(("group", "ep", "tp"), None),
        check_vma=False,
    )
```

time: 120 us -> 63.9 us (0.53)
  matrix products: 34.1 us -> 0 us
  blocking collectives: 28.1 us -> 0 us
  Pallas kernels: 0 us -> 26.6 us
  between operations: 13.5 us -> 0.1 us
  waiting for transfers between devices: 30.1 us -> 20.9 us
  starting transfers between devices: 7.64 us -> 13.5 us
  local copies, waits for them, and re-layouts: 5.67 us -> 1.01 us
    dot_general x7 -> x0, matrix products: 34.1 us -> none  [the longest x1 10.6 us: on_device(): jnp.einsum('rqd,qdf->rqf', piece, w_up, preferred_element_type=jnp.float32)]
    pallas_call x0 -> x2, Pallas kernels: none -> 26.6 us  [the longest x1 25.1 us: experts_of(): pl.pallas_call(functools.partial(expert_kernel, block, rows_dev), out_sha...]
    unnamed x2 -> x0, waiting for transfers between devices: 21.8 us -> none
    ppermute x0 -> x10, waiting for transfers between devices: none -> 20.9 us  [the longest x5 11.1 us: gather(): arrived = [lax.ppermute(rows, axis, partner(count, step)) for step in steps]]
    all_gather x1 -> x0, blocking collectives: 20.3 us -> none  [on_device(): piece = lax.all_gather(packed, 'tp', axis=0, tiled=True)]
    ppermute x0 -> x10, starting transfers between devices: none -> 13.5 us  [the longest x5 7.27 us: gather(): arrived = [lax.ppermute(rows, axis, partner(count, step)) for step in steps]]
    all_to_all x2 -> x0, waiting for transfers between devices: 8.29 us -> none  [the longest x1 4.86 us: on_device(): lax.all_to_all(send_rows, 'ep', split_axis=0, concat_axis=0, tiled=True)]
    all_to_all x1 -> x0, blocking collectives: 7.79 us -> none  [on_device(): lax.all_to_all(returning, 'ep', split_axis=0, concat_axis=0, tiled=True)]
  transfers between devices with their start and end apart: 3 -> 10, of which waited for: 3 -> 8; matrix products, arithmetic and copies ran while one was open for 1% -> 1% of each run, Pallas kernels for 0% -> 0%
where the time goes in v1:
time: 63.9 us; the launch traced here: 63.7 us
  Pallas kernels  26.6 us (42%)
  waiting for transfers between devices  20.9 us (33%)
  starting transfers between devices  13.5 us (21%)
  other arithmetic  1.61 us (3%)
  local copies, waits for them, and re-layouts  1.01 us (2%)
    pallas_call x1, Pallas kernels, experts_of(): pl.pallas_call(functools.partial(expert_kernel, block, rows_dev), out_sha...  25.1 us
    ppermute x5, waiting for transfers between devices, gather(): arrived = [lax.ppermute(rows, axis, partner(count, step)) for step in steps]  11.1 us
    ppermute x5, waiting for transfers between devices, scatter_sum(): lax.ppermute(part, axis, back(count, step))  9.83 us
    ppermute x5, starting transfers between devices, gather(): arrived = [lax.ppermute(rows, axis, partner(count, step)) for step in steps]  7.27 us
    ppermute x5, starting transfers between devices, scatter_sum(): lax.ppermute(part, axis, back(count, step))  6.21 us
    pallas_call x1, Pallas kernels, pack(): pl.pallas_call(functools.partial(pack_kernel, inst_count), out_shape=jax....  1.48 us
  transfers between devices with their start and end apart: 10, of which 8 were waited for; matrix products, arithmetic and copies ran while one was open for 1% of the time, Pallas kernels for 0%

profile of v1, /device:TPU:0, one launch (start us, length us, event | category | flops | bytes accessed | tf_op | source)
XLA Modules:
  0.0 63.7 jit_solution(9314818983937341406)
XLA Ops:
  0.0 1.5 %shard_map.73 = bf16[8,3072]{1,0:T(8,128)(2,1)} custom-call(bf16[6,3072]{1,0:T(8,128)(2,1)} %tokens.1, s32[2,6]{1,0:T(2,128)} %bitcast.4, s32[2,6]{1,0:T(2,128)} %bitcast.5, f32[2,6]{1,0:T(2,128)} %bitcast.6), custom_call_target="tpu_custom_call" | custom-call | tf_op jit(solution)/shard_map/pallas_call | solution.py:81
  1.5 3.1 %collective-permute-start = (bf16[8,3072]{1,0:T(8,128)(2,1)}, bf16[8,3072]{1,0:T(8,128)(2,1)S(1)}, u32[]{:S(2)}, u32[]{:S(2)}) collective-permute-start(bf16[8,3072]{1,0:T(8,128)(2,1)} %shard_map.73), channel_id=1, source_target_pairs={{0,1},{1,0},{2,3},{3,2},{4,5},{5,4},{6,7},{7,6},{8,9},{9,8},{10,11... | collective-permute-start | bytes 147464 | tf_op jit(solution)/shard_map/ppermute | solution.py:38
  4.5 2.6 %collective-permute-start.1 = (bf16[8,3072]{1,0:T(8,128)(2,1)}, bf16[8,3072]{1,0:T(8,128)(2,1)S(1)}, u32[]{:S(2)}, u32[]{:S(2)}) collective-permute-start(bf16[8,3072]{1,0:T(8,128)(2,1)} %shard_map.73), channel_id=1, source_target_pairs={{0,2},{1,3},{2,0},{3,1},{4,6},{5,7},{6,4},{7,5},{8,10},{9,11},{10,... | collective-permute-start | bytes 147464 | tf_op jit(solution)/shard_map/ppermute | solution.py:38
  7.1 0.0 collective-permute-start.2
  7.1 0.9 %constant_dynamic-update-slice_fusion.4 = (bf16[64,3072]{1,0:T(8,128)(2,1)S(1)}, bf16[128,3072]{1,0:T(8,128)(2,1)S(1)}) fusion(bf16[8,3072]{1,0:T(8,128)(2,1)} %shard_map.73), kind=kLoop, calls=%fused_computation.8 | loop fusion | bytes 147456
  8.0 0.0 collective-permute-done
  8.0 2.7 %collective-permute-done.1 = bf16[8,3072]{1,0:T(8,128)(2,1)S(1)} collective-permute-done((bf16[8,3072]{1,0:T(8,128)(2,1)}, bf16[8,3072]{1,0:T(8,128)(2,1)S(1)}, u32[]{:S(2)}, u32[]{:S(2)}) %collective-permute-start.1) | collective-permute-done | bytes 49184 | tf_op jit(solution)/shard_map/ppermute | solution.py:38
  10.7 2.6 %collective-permute-done.2 = bf16[8,3072]{1,0:T(8,128)(2,1)S(1)} collective-permute-done((bf16[8,3072]{1,0:T(8,128)(2,1)}, bf16[8,3072]{1,0:T(8,128)(2,1)S(1)}, u32[]{:S(2)}, u32[]{:S(2)}) %collective-permute-start.2) | collective-permute-done | bytes 49184 | tf_op jit(solution)/shard_map/ppermute | solution.py:38
  13.2 0.8 %pad_maximum_fusion = bf16[32,3072]{1,0:T(8,128)(2,1)S(1)} fusion(bf16[8,3072]{1,0:T(8,128)(2,1)S(1)} %collective-permute-done.2, bf16[8,3072]{1,0:T(8,128)(2,1)S(1)} %collective-permute-done.1, bf16[8,3072]{1,0:T(8,128)(2,1)S(1)} %collective-permute-done, bf16[8,3072]{1,0:T(8,128)(2,1)} %shard_map.73), kind=kLoop, calls=%fused_computation.2 | loop fusion | flops 786432 | bytes 393216 | tf_op jit(solution)/shard_map/concatenate | solution.py:39
  14.0 1.6 %collective-permute-start.3 = (bf16[32,3072]{1,0:T(8,128)(2,1)S(1)}, bf16[32,3072]{1,0:T(8,128)(2,1)S(1)}, u32[]{:S(2)}, u32[]{:S(2)}) collective-permute-start(bf16[32,3072]{1,0:T(8,128)(2,1)S(1)} %pad_maximum_fusion), channel_id=1, source_target_pairs={{0,8},{4,12},{8,0},{12,4},{1,9},{5,13},{9,1},{13,5},{2,10},{6,14},... | collective-permute-start | bytes 589832 | tf_op jit(solution)/shard_map/ppermute | solution.py:38
  15.6 4.1 %collective-permute-done.3 = bf16[32,3072]{1,0:T(8,128)(2,1)S(1)} collective-permute-done((bf16[32,3072]{1,0:T(8,128)(2,1)S(1)}, bf16[32,3072]{1,0:T(8,128)(2,1)S(1)}, u32[]{:S(2)}, u32[]{:S(2)}) %collective-permute-start.3) | collective-permute-done | bytes 196640 | tf_op jit(solution)/shard_map/ppermute | solution.py:38
  19.8 0.1 collective-permute-start.4
  19.9 1.7 %collective-permute-done.4 = bf16[64,3072]{1,0:T(8,128)(2,1)S(1)} collective-permute-done((bf16[64,3072]{1,0:T(8,128)(2,1)S(1)}, bf16[64,3072]{1,0:T(8,128)(2,1)S(1)}, u32[]{:S(2)}, u32[]{:S(2)}) %collective-permute-start.4) | collective-permute-done | bytes 393248 | tf_op jit(solution)/shard_map/ppermute | solution.py:38
  21.6 25.1 %shard_map.74 = bf16[128,3072]{1,0:T(8,128)(2,1)S(1)} custom-call(s32[1]{0:T(128)} %bitcast.first_ref, bf16[128,3072]{1,0:T(8,128)(2,1)S(1)} %constant_dynamic-update-slice_fusion.5.x, bf16[4,3072,1024]{2,1,0:T(8,128)(2,1)} %w_gate.1, bf16[4,3072,1024]{2,1,0:T(8,128)(2,1)} %w_up.1, bf16[4,1024,3072]{2,1,0:T(8,128)(2,1)} %w_down.1), custom_call_target="tpu_custom_call" | custom-call | tf_op jit(solution)/shard_map/pallas_call | solution.py:124
  46.8 0.2 collective-permute-start.5
  47.0 1.6 %collective-permute-done.5 = bf16[64,3072]{1,0:T(8,128)(2,1)S(1)} collective-permute-done((bf16[64,3072]{1,0:T(8,128)(2,1)S(1)}, bf16[64,3072]{1,0:T(8,128)(2,1)S(1)}, u32[]{:S(2)}, u32[]{:S(2)}) %collective-permute-start.5) | collective-permute-done | bytes 393248 | tf_op jit(solution)/shard_map/ppermute | solution.py:48
  48.5 0.1 add_convert_fusion
  48.7 1.6 %collective-permute-start.6 = (bf16[32,3072]{1,0:T(8,128)(2,1)S(1)}, bf16[32,3072]{1,0:T(8,128)(2,1)S(1)}, u32[]{:S(2)}, u32[]{:S(2)}) collective-permute-start(bf16[32,3072]{1,0:T(8,128)(2,1)S(1)} %split.35), channel_id=1, source_target_pairs={{8,0},{12,4},{0,8},{4,12},{9,1},{13,5},{1,9},{5,13},{10,2},{14,6},... | collective-permute-start | bytes 589832 | tf_op jit(solution)/shard_map/ppermute | solution.py:48
  50.2 5.4 %collective-permute-done.6 = bf16[32,3072]{1,0:T(8,128)(2,1)S(1)} collective-permute-done((bf16[32,3072]{1,0:T(8,128)(2,1)S(1)}, bf16[32,3072]{1,0:T(8,128)(2,1)S(1)}, u32[]{:S(2)}, u32[]{:S(2)}) %collective-permute-start.6) | collective-permute-done | bytes 196640 | tf_op jit(solution)/shard_map/ppermute | solution.py:48
  55.8 0.1 collective-permute-start.7
  55.8 1.3 %collective-permute-start.8 = (bf16[8,3072]{1,0:T(8,128)(2,1)S(1)}, bf16[8,3072]{1,0:T(8,128)(2,1)S(1)}, u32[]{:S(2)}, u32[]{:S(2)}) collective-permute-start(bf16[8,3072]{1,0:T(8,128)(2,1)S(1)} %get-tuple-element.7), channel_id=1, source_target_pairs={{2,0},{3,1},{0,2},{1,3},{6,4},{7,5},{4,6},{5,7},{10,8},{11,9},{8,1... | collective-permute-start | bytes 147464 | tf_op jit(solution)/shard_map/ppermute | solution.py:48
  57.1 3.1 %collective-permute-start.9 = (bf16[8,3072]{1,0:T(8,128)(2,1)S(1)}, bf16[8,3072]{1,0:T(8,128)(2,1)S(1)}, u32[]{:S(2)}, u32[]{:S(2)}) collective-permute-start(bf16[8,3072]{1,0:T(8,128)(2,1)S(1)} %get-tuple-element.6), channel_id=1, source_target_pairs={{3,0},{2,1},{1,2},{0,3},{7,4},{6,5},{5,6},{4,7},{11,8},{10,9},{9,1... | collective-permute-start | bytes 147464 | tf_op jit(solution)/shard_map/ppermute | solution.py:48
  60.2 0.0 collective-permute-done.7
  60.2 1.1 %collective-permute-done.8 = bf16[8,3072]{1,0:T(8,128)(2,1)S(1)} collective-permute-done((bf16[8,3072]{1,0:T(8,128)(2,1)S(1)}, bf16[8,3072]{1,0:T(8,128)(2,1)S(1)}, u32[]{:S(2)}, u32[]{:S(2)}) %collective-permute-start.8) | collective-permute-done | bytes 49184 | tf_op jit(solution)/shard_map/ppermute | solution.py:48
  61.4 1.7 %collective-permute-done.9 = bf16[8,3072]{1,0:T(8,128)(2,1)S(1)} collective-permute-done((bf16[8,3072]{1,0:T(8,128)(2,1)S(1)}, bf16[8,3072]{1,0:T(8,128)(2,1)S(1)}, u32[]{:S(2)}, u32[]{:S(2)}) %collective-permute-start.9) | collective-permute-done | bytes 49184 | tf_op jit(solution)/shard_map/ppermute | solution.py:48
  63.0 0.6 %add_convert_fusion.2 = bf16[6,3072]{1,0:T(8,128)(2,1)} fusion(bf16[8,3072]{1,0:T(8,128)(2,1)S(1)} %collective-permute-done.9, bf16[8,3072]{1,0:T(8,128)(2,1)S(1)} %collective-permute-done.8, bf16[8,3072]{1,0:T(8,128)(2,1)S(1)} %collective-permute-done.7, bf16[8,3072]{1,0:T(8,128)(2,1)S(1)} %get-tuple-element.5), kind=kLoop, calls=%fused_computation.3 | loop fusion | flops 147456 | bytes 184320 | tf_op jit(solution)/shard_map/convert_element_type | solution.py:53
  (9 shorter events, 0.2 us)
Async XLA Ops:
  1.5 6.5 %collective-permute-start = (bf16[8,3072]{1,0:T(8,128)(2,1)}, bf16[8,3072]{1,0:T(8,128)(2,1)S(1)}, u32[]{:S(2)}, u32[]{:S(2)}) collective-permute-start(bf16[8,3072]{1,0:T(8,128)(2,1)} %shard_map.73), channel_id=1, source_target_pairs={{0,1},{1,0},{2,3},{3,2},{4,5},{5,4},{6,7},{7,6},{8,9},{9,8},{10,11... | collective-permute-start | bytes 147464 | tf_op jit(solution)/shard_map/ppermute | solution.py:38
  4.5 6.1 %collective-permute-start.1 = (bf16[8,3072]{1,0:T(8,128)(2,1)}, bf16[8,3072]{1,0:T(8,128)(2,1)S(1)}, u32[]{:S(2)}, u32[]{:S(2)}) collective-permute-start(bf16[8,3072]{1,0:T(8,128)(2,1)} %shard_map.73), channel_id=1, source_target_pairs={{0,2},{1,3},{2,0},{3,1},{4,6},{5,7},{6,4},{7,5},{8,10},{9,11},{10,... | collective-permute-start | bytes 147464 | tf_op jit(solution)/shard_map/ppermute | solution.py:38
  7.1 6.1 %collective-permute-start.2 = (bf16[8,3072]{1,0:T(8,128)(2,1)}, bf16[8,3072]{1,0:T(8,128)(2,1)S(1)}, u32[]{:S(2)}, u32[]{:S(2)}) collective-permute-start(bf16[8,3072]{1,0:T(8,128)(2,1)} %shard_map.73), channel_id=1, source_target_pairs={{0,3},{1,2},{2,1},{3,0},{4,7},{5,6},{6,5},{7,4},{8,11},{9,10},{10,... | collective-permute-start | bytes 147464 | tf_op jit(solution)/shard_map/ppermute | solution.py:38
  14.0 5.7 %collective-permute-start.3 = (bf16[32,3072]{1,0:T(8,128)(2,1)S(1)}, bf16[32,3072]{1,0:T(8,128)(2,1)S(1)}, u32[]{:S(2)}, u32[]{:S(2)}) collective-permute-start(bf16[32,3072]{1,0:T(8,128)(2,1)S(1)} %pad_maximum_fusion), channel_id=1, source_target_pairs={{0,8},{4,12},{8,0},{12,4},{1,9},{5,13},{9,1},{13,5},{2,10},{6,14},... | collective-permute-start | bytes 589832 | tf_op jit(solution)/shard_map/ppermute | solution.py:38
  19.8 1.8 %collective-permute-start.4 = (bf16[64,3072]{1,0:T(8,128)(2,1)S(1)}, bf16[64,3072]{1,0:T(8,128)(2,1)S(1)}, u32[]{:S(2)}, u32[]{:S(2)}) collective-permute-start(bf16[64,3072]{1,0:T(8,128)(2,1)S(1)} %get-tuple-element.9), channel_id=1, source_target_pairs={{0,4},{4,0},{8,12},{12,8},{1,5},{5,1},{9,13},{13,9},{2,6},{6,2},{1... | collective-permute-start | bytes 1179656 | tf_op jit(solution)/shard_map/ppermute | solution.py:38
  46.8 1.8 %collective-permute-start.5 = (bf16[64,3072]{1,0:T(8,128)(2,1)S(1)}, bf16[64,3072]{1,0:T(8,128)(2,1)S(1)}, u32[]{:S(2)}, u32[]{:S(2)}) collective-permute-start(bf16[64,3072]{1,0:T(8,128)(2,1)S(1)} %split.33), channel_id=1, source_target_pairs={{4,0},{0,4},{12,8},{8,12},{5,1},{1,5},{13,9},{9,13},{6,2},{2,6},{1... | collective-permute-start | bytes 1179656 | tf_op jit(solution)/shard_map/ppermute | solution.py:48
  48.7 7.0 %collective-permute-start.6 = (bf16[32,3072]{1,0:T(8,128)(2,1)S(1)}, bf16[32,3072]{1,0:T(8,128)(2,1)S(1)}, u32[]{:S(2)}, u32[]{:S(2)}) collective-permute-start(bf16[32,3072]{1,0:T(8,128)(2,1)S(1)} %split.35), channel_id=1, source_target_pairs={{8,0},{12,4},{0,8},{4,12},{9,1},{13,5},{1,9},{5,13},{10,2},{14,6},... | collective-permute-start | bytes 589832 | tf_op jit(solution)/shard_map/ppermute | solution.py:48
  55.8 4.5 %collective-permute-start.7 = (bf16[8,3072]{1,0:T(8,128)(2,1)S(1)}, bf16[8,3072]{1,0:T(8,128)(2,1)S(1)}, u32[]{:S(2)}, u32[]{:S(2)}) collective-permute-start(bf16[8,3072]{1,0:T(8,128)(2,1)S(1)} %get-tuple-element.8), channel_id=1, source_target_pairs={{1,0},{0,1},{3,2},{2,3},{5,4},{4,5},{7,6},{6,7},{9,8},{8,9},{11,10... | collective-permute-start | bytes 147464 | tf_op jit(solution)/shard_map/ppermute | solution.py:48
  55.8 5.5 %collective-permute-start.8 = (bf16[8,3072]{1,0:T(8,128)(2,1)S(1)}, bf16[8,3072]{1,0:T(8,128)(2,1)S(1)}, u32[]{:S(2)}, u32[]{:S(2)}) collective-permute-start(bf16[8,3072]{1,0:T(8,128)(2,1)S(1)} %get-tuple-element.7), channel_id=1, source_target_pairs={{2,0},{3,1},{0,2},{1,3},{6,4},{7,5},{4,6},{5,7},{10,8},{11,9},{8,1... | collective-permute-start | bytes 147464 | tf_op jit(solution)/shard_map/ppermute | solution.py:48
  57.1 5.9 %collective-permute-start.9 = (bf16[8,3072]{1,0:T(8,128)(2,1)S(1)}, bf16[8,3072]{1,0:T(8,128)(2,1)S(1)}, u32[]{:S(2)}, u32[]{:S(2)}) collective-permute-start(bf16[8,3072]{1,0:T(8,128)(2,1)S(1)} %get-tuple-element.6), channel_id=1, source_target_pairs={{3,0},{2,1},{1,2},{0,3},{7,4},{6,5},{5,6},{4,7},{11,8},{10,9},{9,1... | collective-permute-start | bytes 147464 | tf_op jit(solution)/shard_map/ppermute | solution.py:48

commit v2 on v1

v2 whole, which is shorter than its diff:
```python
import functools

import jax
import jax.numpy as jnp
from jax import lax
from jax.experimental import pallas as pl
from jax.experimental.pallas import tpu as pltpu
from jax.sharding import PartitionSpec as P

SPLIT = 2
LANES = 128
META = 2
WIDTH = 512
LOADS = (4, 4)
RING = [4, 2]


def partner(count, step):
    if count & (count - 1) == 0:
        return [(i, i ^ step) for i in range(count)]
    return [(i, (i + step) % count) for i in range(count)]


def back(count, step):
    return [(dst, src) for src, dst in partner(count, step)]


def stages(count, direct):
    if direct or count & (count - 1) != 0:
        return [list(range(1, count))]
    found, bit = [], count // 2
    while bit >= 1:
        found.append([bit])
        bit //= 2
    return found


def gather(rows, axis, direct):
    count = lax.axis_size(axis)
    for steps in stages(count, direct):
        arrived = []
        for step in steps:
            arrived.append(lax.ppermute(rows, axis, partner(count, step)))
        rows = jnp.concatenate([rows] + arrived, axis=0)
    return rows


def scatter_sum(rows, axis, direct):
    count = lax.axis_size(axis)
    for steps in reversed(stages(count, direct)):
        parts = jnp.split(rows, len(steps) + 1, axis=0)
        arrived = [
            lax.ppermute(part, axis, back(count, step)) for part, step in zip(parts[1:], steps)
        ]
        total = parts[0].astype(jnp.float32)
        for part in arrived:
            total = total + part.astype(jnp.float32)
        rows = total.astype(jnp.bfloat16)
    return rows


def pack_kernel(inst_count, tokens, experts, replicas, gates, out, wide):
    rows_dev, _ = tokens.shape
    expert_count = inst_count // 2
    hot_count = expert_count // 2
    wide[...] = jnp.zeros_like(wide)
    wide[:rows_dev, :] = tokens[...].astype(jnp.float32)
    picked, copy = experts[...], replicas[...]
    turn = jnp.zeros_like(picked)
    for e in range(expert_count):
        turn = jnp.where(picked == e, (e - 1) % hot_count, turn)
    instance = jnp.where(copy == 0, picked, expert_count + (copy - 1) * hot_count + turn)
    for i in range(inst_count):
        weight = jnp.sum(jnp.where(instance == i, gates[...], 0.0), axis=0, keepdims=True)
        high = weight.astype(jnp.bfloat16).astype(jnp.float32)
        low = (weight - high).astype(jnp.bfloat16).astype(jnp.float32)
        lanes = slice(i * LANES, i * LANES + rows_dev)
        wide[rows_dev : rows_dev + 1, lanes] = high
        wide[rows_dev + 1 : rows_dev + 2, lanes] = low
    out[...] = wide[...].astype(jnp.bfloat16)


def pack(tokens, experts, replicas, gates, inst_count):
    rows_dev, features = tokens.shape
    block = -(-(rows_dev + META) // 8) * 8
    return pl.pallas_call(
        functools.partial(pack_kernel, inst_count),
        out_shape=jax.ShapeDtypeStruct((block, features), jnp.bfloat16),
        scratch_shapes=[pltpu.VMEM((block, features), jnp.float32)],
        compiler_params=pltpu.CompilerParams(vmem_limit_bytes=2 << 20),
    )(tokens, experts.T, replicas.T, gates.T)


def coef_of(slab, block, rows_dev):
    tile = slab.shape[0]
    shape = (tile // block, block, LANES)
    slab = slab.astype(jnp.float32).reshape(shape)
    weight = slab[:, rows_dev : rows_dev + 1, :] + slab[:, rows_dev + 1 : rows_dev + 2, :]
    row = lax.broadcasted_iota(jnp.int32, shape, 1)
    lane = lax.broadcasted_iota(jnp.int32, shape, 2)
    own = jnp.where((row == lane) & (row < rows_dev), jnp.broadcast_to(weight, shape), 0.0)
    return jnp.sum(own, axis=2, keepdims=True).reshape(tile, 1)


class Plan:
    def __init__(self, w_gate):
        self.pieces, self.features, self.hidden = w_gate.shape
        self.width = min(WIDTH, self.hidden)
        self.parts = self.hidden // self.width
        self.jobs = self.pieces * self.parts
        self.units = 3 * self.jobs
        self.loads, begin = [], 0
        for count in LOADS:
            end = min(begin + count, self.units)
            self.loads.append(range(begin, end))
            begin = end
        self.ready = begin

    def shape(self, unit):
        if unit % 3 == 2:
            return (self.width, self.features)
        return (self.features, self.width)

    def source(self, weights, unit):
        job, kind = unit // 3, unit % 3
        piece, span = job // self.parts, pl.ds(job % self.parts * self.width, self.width)
        if kind == 2:
            return weights[2].at[piece, span, :]
        return weights[kind].at[piece, :, span]


def load_kernel(plan, units, *refs):
    weights, slots, sems = refs[:3], refs[4:-1], refs[-1]
    copies = [
        pltpu.make_async_copy(plan.source(weights, unit), slots[n], sems.at[n])
        for n, unit in enumerate(units)
    ]
    for copy in copies:
        copy.start()
    for copy in copies:
        copy.wait()


def load(plan, index, weights, after):
    units = plan.loads[index]
    if len(units) == 0:
        return []
    anywhere = pl.BlockSpec(memory_space=pltpu.HBM)
    inside = pl.BlockSpec(memory_space=pltpu.VMEM)
    moved = len(units) * plan.features * plan.width * 2
    found = pl.pallas_call(
        functools.partial(load_kernel, plan, units),
        out_shape=[pltpu.VMEM(plan.shape(unit), jnp.bfloat16) for unit in units],
        in_specs=[anywhere] * 3 + [pl.BlockSpec(memory_space=pl.ANY)],
        out_specs=[inside] * len(units),
        scratch_shapes=[pltpu.SemaphoreType.DMA((len(units),))],
        compiler_params=pltpu.CompilerParams(vmem_limit_bytes=1 << 20),
        cost_estimate=pl.CostEstimate(flops=0, bytes_accessed=moved, transcendentals=0),
    )(*weights, after)
    return list(found)


def expert_kernel(plan, block, rows_dev, x, w_gate, w_up, w_down, *refs):
    held, (out, total, wide, tall, sems) = refs[: plan.ready], refs[plan.ready :]
    weights, rings = (w_gate, w_up, w_down), (wide, tall)
    tile = total.shape[0]
    first = lax.axis_index("ep") * plan.pieces
    streams = [
        [u for u in range(plan.ready, plan.units) if u % 3 != 2],
        [u for u in range(plan.ready, plan.units) if u % 3 == 2],
    ]
    depth = [wide.shape[0], tall.shape[0]]
    place = {u: (s, n) for s, units in enumerate(streams) for n, u in enumerate(units)}

    def fetch(unit):
        s, n = place[unit]
        slot = n % depth[s]
        return pltpu.make_async_copy(plan.source(weights, unit), rings[s].at[slot], sems.at[s, slot])

    def use(unit):
        if unit < plan.ready:
            return held[unit]
        fetch(unit).wait()
        s, n = place[unit]
        return rings[s].at[n % depth[s]]

    def free(unit):
        if unit >= plan.ready:
            s, n = place[unit]
            if n + depth[s] < len(streams[s]):
                fetch(streams[s][n + depth[s]]).start()

    def per_tile(r, carry):
        rows = pl.ds(pl.multiple_of(r * tile, tile), tile)
        for unit in range(plan.ready, plan.units):
            s, n = place[unit]
            if n < depth[s]:
                fetch(unit).start()
        for job in range(plan.jobs):
            instance = (first + job // plan.parts) // SPLIT
            lanes = pl.ds(pl.multiple_of(instance * LANES, LANES), LANES)
            coef = coef_of(x[rows, lanes], block, rows_dev)
            gate_act = jnp.dot(x[rows, :], use(3 * job)[...], preferred_element_type=jnp.float32)
            free(3 * job)
            up_act = jnp.dot(x[rows, :], use(3 * job + 1)[...], preferred_element_type=jnp.float32)
            free(3 * job + 1)
            hidden = gate_act / (1.0 + jnp.exp(-gate_act)) * up_act * coef
            share = jnp.dot(
                hidden.astype(jnp.bfloat16),
                use(3 * job + 2)[...],
                preferred_element_type=jnp.float32,
            )
            free(3 * job + 2)
            if job > 0:
                share = total[...] + share
            if job < plan.jobs - 1:
                total[...] = share
            else:
                out[rows, :] = share.astype(jnp.bfloat16)
        return carry

    if x.shape[0] == tile:
        per_tile(0, 0)
    else:
        lax.fori_loop(0, x.shape[0] // tile, per_tile, 0)


def experts_of(plan, x, weights, held, block, rows_dev):
    rows, features = x.shape
    tile = min(rows, 128)
    anywhere = pl.BlockSpec(memory_space=pltpu.HBM)
    inside = pl.BlockSpec(memory_space=pltpu.VMEM)
    held = [pltpu.with_memory_space_constraint(unit, pltpu.VMEM) for unit in held]
    limit = 4 << 20
    depth = [1, 1]
    if plan.ready < plan.units:
        depth = RING
    limit += sum(depth) * plan.width * features * 2
    return pl.pallas_call(
        functools.partial(expert_kernel, plan, block, rows_dev),
        out_shape=jax.ShapeDtypeStruct((rows, features), jnp.bfloat16),
        in_specs=[inside] + [anywhere] * 3 + [inside] * len(held),
        out_specs=inside,
        scratch_shapes=[
            pltpu.VMEM((tile, features), jnp.float32),
            pltpu.VMEM((depth[0], features, plan.width), jnp.bfloat16),
            pltpu.VMEM((depth[1], plan.width, features), jnp.bfloat16),
            pltpu.SemaphoreType.DMA((2, max(depth))),
        ],
        compiler_params=pltpu.CompilerParams(vmem_limit_bytes=limit),
    )(x, *weights, *held)


def on_device(tokens, experts, replicas, gates, w_gate, w_up, w_down):
    plan = Plan(w_gate)
    weights = [pltpu.with_memory_space_constraint(w, pltpu.HBM) for w in (w_gate, w_up, w_down)]
    inst_count = plan.pieces * lax.axis_size("ep") // SPLIT
    rows_dev = tokens.shape[0]
    direct = lax.axis_size("tp") <= 4
    block_rows = pack(tokens, experts, replicas, gates, inst_count)
    block = block_rows.shape[0]
    held = load(plan, 0, weights, block_rows)
    rows = gather(block_rows, "tp", direct)
    held = held + load(plan, 1, weights, rows)
    rows = gather(rows, "ep", False)
    share = experts_of(plan, rows, weights, held, block, rows_dev)
    share = scatter_sum(share, "ep", False)
    share = scatter_sum(share, "tp", direct)
    return share[:rows_dev]


def solution(mesh):
    return jax.shard_map(
        on_device,
        mesh=mesh,
        in_specs=(
            P(("group", "ep", "tp"), None),
            P(("group", "ep", "tp"), None),
            P(("group", "ep", "tp"), None),
            P(("group", "ep", "tp"), None),
            P("ep", None, "tp"),
            P("ep", None, "tp"),
            P("ep", "tp", None),
        ),
        out_specs=P(("group", "ep", "tp"), None),
        check_vma=False,
    )
```

time: 63.9 us -> 64.6 us (1.011)
  waiting for transfers between devices: 20.9 us -> 18.7 us
  local copies, waits for them, and re-layouts: 1.01 us -> 2.98 us
  Pallas kernels: 26.6 us -> 27.8 us
  other arithmetic: 1.61 us -> 0.81 us
    pallas_call x1 -> x3, Pallas kernels: 25.1 us -> 27.8 us  [the longest x1 18.1 us: experts_of(): pl.pallas_call(functools.partial(expert_kernel, plan, block, rows_dev), o...]
    ppermute x5, waiting for transfers between devices: 11.1 us -> 8.57 us  [gather(): arrived.append(lax.ppermute(rows, axis, partner(count, step)))]
    unnamed x4 -> x12, local copies, waits for them, and re-layouts: 0.89 us -> 2.86 us
    pallas_call x1, Pallas kernels: 1.48 us -> 0.04 us  [pack(): pl.pallas_call(functools.partial(pack_kernel, inst_count), out_shape=jax....]
    concatenate x1, other arithmetic: 0.81 us -> 0.01 us  [gather(): rows = jnp.concatenate([rows] + arrived, axis=0)]
  transfers between devices with their start and end apart: 10 -> 10, of which waited for: 8 -> 7; matrix products, arithmetic and copies ran while one was open for 1% -> 0% of each run, Pallas kernels for 0% -> 15%
where the time goes in v2:
time: 64.6 us; the launch traced here: 64.4 us
  Pallas kernels  27.8 us (43%)
  waiting for transfers between devices  18.7 us (29%)
  starting transfers between devices  14 us (22%)
  local copies, waits for them, and re-layouts  2.98 us (5%)
  other arithmetic  0.81 us (1%)
    pallas_call x1, Pallas kernels, experts_of(): pl.pallas_call(functools.partial(expert_kernel, plan, block, rows_dev), o...  18.1 us
    ppermute x5, waiting for transfers between devices, scatter_sum(): lax.ppermute(part, axis, back(count, step))  10.2 us
    pallas_call x2, Pallas kernels, load(): pl.pallas_call(functools.partial(load_kernel, plan, units), out_shape=[pl...  9.65 us
    ppermute x5, waiting for transfers between devices, gather(): arrived.append(lax.ppermute(rows, axis, partner(count, step)))  8.57 us
    ppermute x5, starting transfers between devices, gather(): arrived.append(lax.ppermute(rows, axis, partner(count, step)))  7.41 us
    ppermute x5, starting transfers between devices, scatter_sum(): lax.ppermute(part, axis, back(count, step))  6.56 us
    unnamed x12, local copies, waits for them, and re-layouts  2.86 us
  transfers between devices with their start and end apart: 10, of which 7 were waited for; matrix products, arithmetic and copies ran while one was open for 0% of the time, Pallas kernels for 15%

profile of v2, /device:TPU:0, one launch (start us, length us, event | category | flops | bytes accessed | tf_op | source)
XLA Modules:
  0.0 64.4 jit_solution(15377464399105383668)
XLA Ops:
  0.0 0.0 copy-start
  0.0 0.8 %copy-done = bf16[6,3072]{1,0:T(8,128)(2,1)S(1)} copy-done((bf16[6,3072]{1,0:T(8,128)(2,1)S(1)}, bf16[6,3072]{1,0:T(8,128)(2,1)}, u32[]{:S(2)}) %copy-start) | copy-done | bytes 36888
  0.8 0.0 copy-start.1
  0.8 0.7 %copy-done.1 = s32[6,2]{0,1:T(2,128)S(1)} copy-done((s32[6,2]{0,1:T(2,128)S(1)}, s32[6,2]{0,1:T(2,128)}, u32[]{:S(2)}) %copy-start.1) | copy-done | bytes 72
  1.5 0.0 copy-start.2
  1.5 0.7 %copy-done.2 = s32[6,2]{0,1:T(2,128)S(1)} copy-done((s32[6,2]{0,1:T(2,128)S(1)}, s32[6,2]{0,1:T(2,128)}, u32[]{:S(2)}) %copy-start.2) | copy-done | bytes 72
  2.2 0.0 copy-start.3
  2.2 0.7 %copy-done.3 = f32[6,2]{0,1:T(2,128)S(1)} copy-done((f32[6,2]{0,1:T(2,128)S(1)}, f32[6,2]{0,1:T(2,128)}, u32[]{:S(2)}) %copy-start.3) | copy-done | bytes 72
  2.9 5.1 %collective-permute-start.2 = (bf16[8,3072]{1,0:T(8,128)(2,1)S(1)}, bf16[8,3072]{1,0:T(8,128)(2,1)S(1)}, u32[]{:S(2)}, u32[]{:S(2)}) collective-permute-start(bf16[8,3072]{1,0:T(8,128)(2,1)S(1)} %shard_map.73.refs_3_), channel_id=1, source_target_pairs={{0,3},{1,2},{2,1},{3,0},{4,7},{5,6},{6,5},{7,4},{8,11},{9,10},{10,... | collective-permute-start | bytes 147464 | tf_op jit(solution)/shard_map/ppermute | solution.py:43
  8.0 0.0 collective-permute-start.1
  8.0 0.6 collective-permute-start
  8.7 1.5 %collective-permute-done.2 = bf16[8,3072]{1,0:T(8,128)(2,1)S(1)} collective-permute-done((bf16[8,3072]{1,0:T(8,128)(2,1)S(1)}, bf16[8,3072]{1,0:T(8,128)(2,1)S(1)}, u32[]{:S(2)}, u32[]{:S(2)}) %collective-permute-start.2) | collective-permute-done | bytes 49184 | tf_op jit(solution)/shard_map/ppermute | solution.py:43
  10.2 2.9 %collective-permute-done.1 = bf16[8,3072]{1,0:T(8,128)(2,1)S(1)} collective-permute-done((bf16[8,3072]{1,0:T(8,128)(2,1)S(1)}, bf16[8,3072]{1,0:T(8,128)(2,1)S(1)}, u32[]{:S(2)}, u32[]{:S(2)}) %collective-permute-start.1) | collective-permute-done | bytes 49184 | tf_op jit(solution)/shard_map/ppermute | solution.py:43
  13.0 0.0 collective-permute-done
  13.0 1.6 %collective-permute-start.3 = (bf16[32,3072]{1,0:T(8,128)(2,1)S(1)}, bf16[32,3072]{1,0:T(8,128)(2,1)S(1)}, u32[]{:S(2)}, u32[]{:S(2)}) collective-permute-start(bf16[32,3072]{1,0:T(8,128)(2,1)S(1)} %pad_maximum_fusion.refs_3_), channel_id=1, source_target_pairs={{0,8},{4,12},{8,0},{12,4},{1,9},{5,13},{9,1},{13,5},{2,10},{6,14},... | collective-permute-start | bytes 589832 | tf_op jit(solution)/shard_map/ppermute | solution.py:43
  14.6 4.2 %collective-permute-done.3 = bf16[32,3072]{1,0:T(8,128)(2,1)S(1)} collective-permute-done((bf16[32,3072]{1,0:T(8,128)(2,1)S(1)}, bf16[32,3072]{1,0:T(8,128)(2,1)S(1)}, u32[]{:S(2)}, u32[]{:S(2)}) %collective-permute-start.3) | collective-permute-done | bytes 196640 | tf_op jit(solution)/shard_map/ppermute | solution.py:43
  18.9 0.1 collective-permute-start.4
  19.0 4.7 %shard_map.74 = (bf16[3072,512]{1,0:T(8,128)(2,1)S(1)}, bf16[3072,512]{1,0:T(8,128)(2,1)S(1)}, bf16[512,3072]{1,0:T(8,128)(2,1)S(1)}, bf16[3072,512]{1,0:T(8,128)(2,1)S(1)}) custom-call(bf16[4,3072,1024]{2,1,0:T(8,128)(2,1)} %w_gate.1, bf16[4,3072,1024]{2,1,0:T(8,128)(2,1)} %w_up.1, bf16[4,1024,3072]{2,1,0:T(8,128)(2,1)} %w_down.1, ...), custom_call_target="tpu_custom_call" | custom-call | bytes 12582912 | tf_op jit(solution)/shard_map/pallas_call | solution.py:151
  23.7 5.0 %shard_map.75 = (bf16[3072,512]{1,0:T(8,128)(2,1)S(1)}, bf16[512,3072]{1,0:T(8,128)(2,1)S(1)}, bf16[3072,512]{1,0:T(8,128)(2,1)S(1)}, bf16[3072,512]{1,0:T(8,128)(2,1)S(1)}) custom-call(bf16[4,3072,1024]{2,1,0:T(8,128)(2,1)} %w_gate.1, bf16[4,3072,1024]{2,1,0:T(8,128)(2,1)} %w_up.1, bf16[4,1024,3072]{2,1,0:T(8,128)(2,1)} %w_down.1, ...), custom_call_target="tpu_custom_call" | custom-call | bytes 12582912 | tf_op jit(solution)/shard_map/pallas_call | solution.py:151
  28.6 0.0 collective-permute-done.4
  28.7 18.1 %shard_map.76 = bf16[128,3072]{1,0:T(8,128)(2,1)S(1)} custom-call(bf16[128,3072]{1,0:T(8,128)(2,1)S(1)} %constant_dynamic-update-slice_fusion.5.x, bf16[4,3072,1024]{2,1,0:T(8,128)(2,1)} %w_gate.1, bf16[4,3072,1024]{2,1,0:T(8,128)(2,1)} %w_up.1, bf16[4,1024,3072]{2,1,0:T(8,128)(2,1)} %w_down.1, bf16[3072,512]{1,0:T(8,128)(2,1)S(1)} %get-tuple-element.13.refs_0_, ...), custom_call_target="tpu_custom_call" | custom-call | tf_op jit(solution)/shard_map/pallas_call | solution.py:239
  46.8 0.6 collective-permute-start.5
  47.4 1.3 %collective-permute-done.5 = bf16[64,3072]{1,0:T(8,128)(2,1)S(1)} collective-permute-done((bf16[64,3072]{1,0:T(8,128)(2,1)S(1)}, bf16[64,3072]{1,0:T(8,128)(2,1)S(1)}, u32[]{:S(2)}, u32[]{:S(2)}) %collective-permute-start.5) | collective-permute-done | bytes 393248 | tf_op jit(solution)/shard_map/ppermute | solution.py:53
  48.7 0.1 add_convert_fusion
  48.9 1.6 %collective-permute-start.6 = (bf16[32,3072]{1,0:T(8,128)(2,1)S(1)}, bf16[32,3072]{1,0:T(8,128)(2,1)S(1)}, u32[]{:S(2)}, u32[]{:S(2)}) collective-permute-start(bf16[32,3072]{1,0:T(8,128)(2,1)S(1)} %split.35), channel_id=1, source_target_pairs={{8,0},{12,4},{0,8},{4,12},{9,1},{13,5},{1,9},{5,13},{10,2},{14,6},... | collective-permute-start | bytes 589832 | tf_op jit(solution)/shard_map/ppermute | solution.py:53
  50.4 5.7 %collective-permute-done.6 = bf16[32,3072]{1,0:T(8,128)(2,1)S(1)} collective-permute-done((bf16[32,3072]{1,0:T(8,128)(2,1)S(1)}, bf16[32,3072]{1,0:T(8,128)(2,1)S(1)}, u32[]{:S(2)}, u32[]{:S(2)}) %collective-permute-start.6) | collective-permute-done | bytes 196640 | tf_op jit(solution)/shard_map/ppermute | solution.py:53
  56.2 2.1 %collective-permute-start.9 = (bf16[8,3072]{1,0:T(8,128)(2,1)S(1)}, bf16[8,3072]{1,0:T(8,128)(2,1)S(1)}, u32[]{:S(2)}, u32[]{:S(2)}) collective-permute-start(bf16[8,3072]{1,0:T(8,128)(2,1)S(1)} %get-tuple-element.22), channel_id=1, source_target_pairs={{3,0},{2,1},{1,2},{0,3},{7,4},{6,5},{5,6},{4,7},{11,8},{10,9},{9,1... | collective-permute-start | bytes 147464 | tf_op jit(solution)/shard_map/ppermute | solution.py:53
  58.3 0.2 collective-permute-start.8
  58.4 2.2 %collective-permute-start.7 = (bf16[8,3072]{1,0:T(8,128)(2,1)S(1)}, bf16[8,3072]{1,0:T(8,128)(2,1)S(1)}, u32[]{:S(2)}, u32[]{:S(2)}) collective-permute-start(bf16[8,3072]{1,0:T(8,128)(2,1)S(1)} %get-tuple-element.24), channel_id=1, source_target_pairs={{1,0},{0,1},{3,2},{2,3},{5,4},{4,5},{7,6},{6,7},{9,8},{8,9},{11,10... | collective-permute-start | bytes 147464 | tf_op jit(solution)/shard_map/ppermute | solution.py:53
  60.6 1.5 %collective-permute-done.9 = bf16[8,3072]{1,0:T(8,128)(2,1)S(1)} collective-permute-done((bf16[8,3072]{1,0:T(8,128)(2,1)S(1)}, bf16[8,3072]{1,0:T(8,128)(2,1)S(1)}, u32[]{:S(2)}, u32[]{:S(2)}) %collective-permute-start.9) | collective-permute-done | bytes 49184 | tf_op jit(solution)/shard_map/ppermute | solution.py:53
  62.1 1.6 %collective-permute-done.8 = bf16[8,3072]{1,0:T(8,128)(2,1)S(1)} collective-permute-done((bf16[8,3072]{1,0:T(8,128)(2,1)S(1)}, bf16[8,3072]{1,0:T(8,128)(2,1)S(1)}, u32[]{:S(2)}, u32[]{:S(2)}) %collective-permute-start.8) | collective-permute-done | bytes 49184 | tf_op jit(solution)/shard_map/ppermute | solution.py:53
  63.8 0.0 collective-permute-done.7
  63.8 0.6 %add_convert_fusion.2 = bf16[6,3072]{1,0:T(8,128)(2,1)} fusion(bf16[8,3072]{1,0:T(8,128)(2,1)S(1)} %collective-permute-done.9, bf16[8,3072]{1,0:T(8,128)(2,1)S(1)} %collective-permute-done.8, bf16[8,3072]{1,0:T(8,128)(2,1)S(1)} %collective-permute-done.7, bf16[8,3072]{1,0:T(8,128)(2,1)S(1)} %get-tuple-element.21), kind=kLoop, calls=%fused_computation.3 | loop fusion | flops 147456 | bytes 184320 | tf_op jit(solution)/shard_map/convert_element_type | solution.py:58
  (12 shorter events, 0.2 us)
Async XLA Ops:
  0.0 0.8 %copy-start = (bf16[6,3072]{1,0:T(8,128)(2,1)S(1)}, bf16[6,3072]{1,0:T(8,128)(2,1)}, u32[]{:S(2)}) copy-start(bf16[6,3072]{1,0:T(8,128)(2,1)} %tokens.1) | copy-start | bytes 110596
  0.8 0.7 %copy-start.1 = (s32[6,2]{0,1:T(2,128)S(1)}, s32[6,2]{0,1:T(2,128)}, u32[]{:S(2)}) copy-start(s32[6,2]{0,1:T(2,128)} %param.8) | copy-start | bytes 148
  1.5 0.7 %copy-start.2 = (s32[6,2]{0,1:T(2,128)S(1)}, s32[6,2]{0,1:T(2,128)}, u32[]{:S(2)}) copy-start(s32[6,2]{0,1:T(2,128)} %param.9) | copy-start | bytes 148
  2.2 0.7 %copy-start.3 = (f32[6,2]{0,1:T(2,128)S(1)}, f32[6,2]{0,1:T(2,128)}, u32[]{:S(2)}) copy-start(f32[6,2]{0,1:T(2,128)} %param.10) | copy-start | bytes 148
  2.9 7.3 %collective-permute-start.2 = (bf16[8,3072]{1,0:T(8,128)(2,1)S(1)}, bf16[8,3072]{1,0:T(8,128)(2,1)S(1)}, u32[]{:S(2)}, u32[]{:S(2)}) collective-permute-start(bf16[8,3072]{1,0:T(8,128)(2,1)S(1)} %shard_map.73.refs_3_), channel_id=1, source_target_pairs={{0,3},{1,2},{2,1},{3,0},{4,7},{5,6},{6,5},{7,4},{8,11},{9,10},{10,... | collective-permute-start | bytes 147464 | tf_op jit(solution)/shard_map/ppermute | solution.py:43
  8.0 5.0 %collective-permute-start.1 = (bf16[8,3072]{1,0:T(8,128)(2,1)S(1)}, bf16[8,3072]{1,0:T(8,128)(2,1)S(1)}, u32[]{:S(2)}, u32[]{:S(2)}) collective-permute-start(bf16[8,3072]{1,0:T(8,128)(2,1)S(1)} %shard_map.73.refs_3_), channel_id=1, source_target_pairs={{0,2},{1,3},{2,0},{3,1},{4,6},{5,7},{6,4},{7,5},{8,10},{9,11},{10,... | collective-permute-start | bytes 147464 | tf_op jit(solution)/shard_map/ppermute | solution.py:43
  8.0 5.0 %collective-permute-start = (bf16[8,3072]{1,0:T(8,128)(2,1)S(1)}, bf16[8,3072]{1,0:T(8,128)(2,1)S(1)}, u32[]{:S(2)}, u32[]{:S(2)}) collective-permute-start(bf16[8,3072]{1,0:T(8,128)(2,1)S(1)} %shard_map.73.refs_3_), channel_id=1, source_target_pairs={{0,1},{1,0},{2,3},{3,2},{4,5},{5,4},{6,7},{7,6},{8,9},{9,8},{10,11... | collective-permute-start | bytes 147464 | tf_op jit(solution)/shard_map/ppermute | solution.py:43
  13.0 5.8 %collective-permute-start.3 = (bf16[32,3072]{1,0:T(8,128)(2,1)S(1)}, bf16[32,3072]{1,0:T(8,128)(2,1)S(1)}, u32[]{:S(2)}, u32[]{:S(2)}) collective-permute-start(bf16[32,3072]{1,0:T(8,128)(2,1)S(1)} %pad_maximum_fusion.refs_3_), channel_id=1, source_target_pairs={{0,8},{4,12},{8,0},{12,4},{1,9},{5,13},{9,1},{13,5},{2,10},{6,14},... | collective-permute-start | bytes 589832 | tf_op jit(solution)/shard_map/ppermute | solution.py:43
  18.9 9.7 %collective-permute-start.4 = (bf16[64,3072]{1,0:T(8,128)(2,1)S(1)}, bf16[64,3072]{1,0:T(8,128)(2,1)S(1)}, u32[]{:S(2)}, u32[]{:S(2)}) collective-permute-start(bf16[64,3072]{1,0:T(8,128)(2,1)S(1)} %get-tuple-element.25), channel_id=1, source_target_pairs={{0,4},{4,0},{8,12},{12,8},{1,5},{5,1},{9,13},{13,9},{2,6},{6,2},{1... | collective-permute-start | bytes 1179656 | tf_op jit(solution)/shard_map/ppermute | solution.py:43
  46.8 1.9 %collective-permute-start.5 = (bf16[64,3072]{1,0:T(8,128)(2,1)S(1)}, bf16[64,3072]{1,0:T(8,128)(2,1)S(1)}, u32[]{:S(2)}, u32[]{:S(2)}) collective-permute-start(bf16[64,3072]{1,0:T(8,128)(2,1)S(1)} %split.33), channel_id=1, source_target_pairs={{4,0},{0,4},{12,8},{8,12},{5,1},{1,5},{13,9},{9,13},{6,2},{2,6},{1... | collective-permute-start | bytes 1179656 | tf_op jit(solution)/shard_map/ppermute | solution.py:53
  48.9 7.2 %collective-permute-start.6 = (bf16[32,3072]{1,0:T(8,128)(2,1)S(1)}, bf16[32,3072]{1,0:T(8,128)(2,1)S(1)}, u32[]{:S(2)}, u32[]{:S(2)}) collective-permute-start(bf16[32,3072]{1,0:T(8,128)(2,1)S(1)} %split.35), channel_id=1, source_target_pairs={{8,0},{12,4},{0,8},{4,12},{9,1},{13,5},{1,9},{5,13},{10,2},{14,6},... | collective-permute-start | bytes 589832 | tf_op jit(solution)/shard_map/ppermute | solution.py:53
  56.2 6.0 %collective-permute-start.9 = (bf16[8,3072]{1,0:T(8,128)(2,1)S(1)}, bf16[8,3072]{1,0:T(8,128)(2,1)S(1)}, u32[]{:S(2)}, u32[]{:S(2)}) collective-permute-start(bf16[8,3072]{1,0:T(8,128)(2,1)S(1)} %get-tuple-element.22), channel_id=1, source_target_pairs={{3,0},{2,1},{1,2},{0,3},{7,4},{6,5},{5,6},{4,7},{11,8},{10,9},{9,1... | collective-permute-start | bytes 147464 | tf_op jit(solution)/shard_map/ppermute | solution.py:53
  58.3 5.5 %collective-permute-start.8 = (bf16[8,3072]{1,0:T(8,128)(2,1)S(1)}, bf16[8,3072]{1,0:T(8,128)(2,1)S(1)}, u32[]{:S(2)}, u32[]{:S(2)}) collective-permute-start(bf16[8,3072]{1,0:T(8,128)(2,1)S(1)} %get-tuple-element.23), channel_id=1, source_target_pairs={{2,0},{3,1},{0,2},{1,3},{6,4},{7,5},{4,6},{5,7},{10,8},{11,9},{8,1... | collective-permute-start | bytes 147464 | tf_op jit(solution)/shard_map/ppermute | solution.py:53
  58.4 5.3 %collective-permute-start.7 = (bf16[8,3072]{1,0:T(8,128)(2,1)S(1)}, bf16[8,3072]{1,0:T(8,128)(2,1)S(1)}, u32[]{:S(2)}, u32[]{:S(2)}) collective-permute-start(bf16[8,3072]{1,0:T(8,128)(2,1)S(1)} %get-tuple-element.24), channel_id=1, source_target_pairs={{1,0},{0,1},{3,2},{2,3},{5,4},{4,5},{7,6},{6,7},{9,8},{8,9},{11,10... | collective-permute-start | bytes 147464 | tf_op jit(solution)/shard_map/ppermute | solution.py:53
